TPU v7x, 512 devices: a whole 4x4x16 slice. The times are simulated.
512 devices in a mesh: group: 64 (over x_lo, z, core), shard: 8 (over y, x_hi).
Axes of the slice: x: 4 (x_hi: 2, x_lo: 2; x = x_hi * 2 + x_lo), y: 4, z: 16, core: 2. Of those that a mesh axis runs over, the one named last changes fastest.
Arguments:
- prompts: bfloat16 [512, 128, 1280], P(('group', 'shard')), may hold values from -6 to 6
- lengths: int32 [512], P(('group', 'shard')), may hold values from 32 to 128
- qkv_master: float32 [1280, 1920], P('group', 'shard')
- out_master: float32 [1280, 1280], P('group', 'shard'), may hold values from -0.15625 to 0.15625
- gate_up_master: float32 [1280, 2, 3584], P('group', None, 'shard'), may hold values from -0.15625 to 0.15625
- down_weight: bfloat16 [3584, 1280], P('shard'), may hold values from -0.09375 to 0.09375
- attn_gain: float32 [1280], replicated, may hold values from 0.25 to 1.75
- mlp_gain: float32 [1280], replicated, may hold values from 0.25 to 1.75
Outputs:
- hidden: bfloat16 [512, 128, 1280], P(('group', 'shard'))
- cache: bfloat16 [512, 128, 640], P(('group', 'shard'))
Inputs may be any that keep to these rules, and one draw needn't show every extreme that they name: `lengths`: live tokens of each prompt; positions from the length on are padding.
All inputs are finite; a program needn't handle non-finite values.
Results may differ from a plain program's by a relative error of at most 0.013.
The roundings to bfloat16 on the way count: a program that leaves them out, or rounds other values in their place, can miss the bound.
Values may be sent and summed in bfloat16 or wider, within the bound.
No kernel may reach another device: no remote copies, remote signals or barrier semaphores. Data moves between devices by JAX's collectives and lax.ppermute only.
A program may use at most 64 MiB of HBM per device.

v0:
```python
import jax
import jax.numpy as jnp
from jax import lax
from jax.sharding import PartitionSpec as P

QUERY_HEADS = 20
KEY_VALUE_HEADS = 5
HEAD_SIZE = 64


def norm_rows(stream, scale_gain):
    return (
        stream * lax.rsqrt(jnp.mean(stream * stream, axis=-1, keepdims=True) + 1e-05) * scale_gain
    )


def rotary(heads, positions):
    half_dim = heads.shape[-1] // 2
    frequency = 10000.0 ** (-(jnp.arange(half_dim).astype(heads.dtype) * 2.0 / heads.shape[-1]))
    angles = positions[:, None] * frequency[None, :]
    cosine = jnp.cos(angles)[:, None, :]
    sine_part = jnp.sin(angles)[:, None, :]
    first_half = heads[..., :half_dim]
    second_half = heads[..., half_dim:]
    return jnp.concatenate(
        [
            first_half * cosine - second_half * sine_part,
            second_half * cosine + first_half * sine_part,
        ],
        axis=-1,
    )


def attention(query_key_value, length):
    token_rows = query_key_value.shape[0]
    query = (
        query_key_value[:, : QUERY_HEADS * HEAD_SIZE]
        .astype(jnp.float32)
        .reshape(token_rows, QUERY_HEADS, HEAD_SIZE)
    )
    key_rows = (
        query_key_value[:, QUERY_HEADS * HEAD_SIZE : (QUERY_HEADS + KEY_VALUE_HEADS) * HEAD_SIZE]
        .astype(jnp.float32)
        .reshape(token_rows, KEY_VALUE_HEADS, HEAD_SIZE)
    )
    value_rows = query_key_value[:, (QUERY_HEADS + KEY_VALUE_HEADS) * HEAD_SIZE :].reshape(
        token_rows, KEY_VALUE_HEADS, HEAD_SIZE
    )
    positions = jnp.arange(token_rows).astype(jnp.float32)
    rotated_query = rotary(query, positions).astype(jnp.bfloat16)
    rotated_keys = rotary(key_rows, positions).astype(jnp.bfloat16)
    grouped_queries = rotated_query.reshape(
        token_rows, KEY_VALUE_HEADS, QUERY_HEADS // KEY_VALUE_HEADS, HEAD_SIZE
    )
    scores = jnp.einsum(
        "qkgd,skd->kgqs", grouped_queries, rotated_keys, preferred_element_type=jnp.float32
    ) * HEAD_SIZE ** (-0.5)
    indices = jnp.arange(token_rows)
    allowed = (indices[None, :] <= indices[:, None]) & (indices[None, :] < length)
    scores = jnp.where(allowed, scores, -1e30)
    largest = jnp.max(scores, axis=-1, keepdims=True)
    weights = jnp.exp(scores - largest)
    probability = (weights / jnp.sum(weights, axis=-1, keepdims=True)).astype(jnp.bfloat16)
    attended = jnp.einsum(
        "kgqs,skd->qkgd", probability, value_rows, preferred_element_type=jnp.float32
    )
    return (
        attended.reshape(token_rows, QUERY_HEADS * HEAD_SIZE).astype(jnp.bfloat16),
        rotated_keys,
        value_rows,
    )


def fold_rows(left, blocks):
    summed = jnp.dot(left, blocks[0], preferred_element_type=jnp.float32)
    placed = blocks[1]
    return (summed, placed)


def fold_units(left, block_rows):
    span_rows = block_rows.shape[0]
    return jnp.dot(left, block_rows.reshape(span_rows, -1), preferred_element_type=jnp.float32)


def shards(
    prompts, lengths, qkv_master, out_master, gate_up_master, down_weight, attn_gain, mlp_gain
):
    stream = prompts[0].astype(jnp.float32)
    token_rows = stream.shape[0]
    length = lengths[0]
    normed_in = norm_rows(stream, attn_gain).astype(jnp.bfloat16)
    qkv_columns, out_columns = (
        lax.all_gather(qkv_master.astype(jnp.bfloat16), "shard", axis=1, tiled=True),
        lax.all_gather(out_master.astype(jnp.bfloat16), "shard", axis=1, tiled=True),
    )
    summed, w_out = fold_rows(
        normed_in,
        (
            lax.all_gather(qkv_columns, "group", axis=0, tiled=True),
            lax.all_gather(out_columns, "group", axis=0, tiled=True),
        ),
    )
    query_key_value = summed.astype(jnp.bfloat16)
    attended, rotated_keys, value_rows = attention(query_key_value, length)
    middle = stream + jnp.dot(attended, w_out, preferred_element_type=jnp.float32)
    normed_mid = norm_rows(middle, mlp_gain).astype(jnp.bfloat16)
    gathered_mid = lax.all_gather(normed_mid, "shard", axis=0, tiled=True)
    units = gate_up_master.shape[2]
    summed_units = fold_units(
        gathered_mid,
        lax.all_gather(gate_up_master.astype(jnp.bfloat16), "group", axis=0, tiled=True),
    )
    gate_up = summed_units.reshape(-1, 2, units)
    hidden_units = (jax.nn.silu(gate_up[:, 0]) * gate_up[:, 1]).astype(jnp.bfloat16)
    feed_out = lax.psum_scatter(
        jnp.dot(hidden_units, down_weight, preferred_element_type=jnp.float32).astype(jnp.bfloat16),
        "shard",
        scatter_dimension=0,
        tiled=True,
    ).astype(jnp.float32)
    live_rows = (jnp.arange(token_rows) < length).astype(jnp.float32)[:, None]
    hidden = (live_rows * (middle + feed_out)).astype(jnp.bfloat16)
    joined_heads = jnp.concatenate(
        [
            rotated_keys.reshape(token_rows, KEY_VALUE_HEADS * HEAD_SIZE).astype(jnp.float32),
            value_rows.reshape(token_rows, KEY_VALUE_HEADS * HEAD_SIZE).astype(jnp.float32),
        ],
        axis=-1,
    )
    cache = (live_rows * joined_heads).astype(jnp.bfloat16)
    return (hidden[None], cache[None])


def solution(mesh):
    in_specs = (
        P(("group", "shard"), None, None),
        P(("group", "shard")),
        P("group", "shard"),
        P("group", "shard"),
        P("group", None, "shard"),
        P("shard", None),
        P(),
        P(),
    )
    out_specs = (P(("group", "shard"), None, None), P(("group", "shard"), None, None))
    return jax.shard_map(shards, mesh=mesh, in_specs=in_specs, out_specs=out_specs, check_vma=False)
```

profile of v0, /device:TPU:32, one launch (start us, length us, event | category | flops | bytes accessed | tf_op | source)
XLA Modules:
  0.0 599.7 jit_solution(9727599761350218476)
XLA Ops:
  7.2 0.0 copy-start
  7.2 0.0 all-gather.15.cloned.1.call-start
  7.2 0.8 convert_bitcast_fusion
  8.1 34.6 %all-gather.2 = bf16[8,160,20]{1,2,0:T(8,128)(2,1)S(1)} all-gather(bf16[1,160,20]{1,2,0:T(8,128)(2,1)S(1)} %convert_bitcast_fusion), channel_id=1, replica_groups=mesh['group'=64,'shard'=8] {'shard'}, dimensions={0}, use_global_device_ids=true | all-gather | bytes 57600 | tf_op jit(solution)/shard_map/all_gather | solution.py:94
  42.6 0.8 reshape.195
  43.4 0.0 all-gather.15.cloned.1.call-update
  43.4 0.0 all-gather.13.cloned.1.call-start
  43.5 0.7 convert_bitcast_fusion.1
  44.2 34.2 %all-gather = bf16[8,240,20]{1,2,0:T(8,128)(2,1)S(1)} all-gather(bf16[1,240,20]{1,2,0:T(8,128)(2,1)S(1)} %convert_bitcast_fusion.1), channel_id=1, replica_groups=mesh['group'=64,'shard'=8] {'shard'}, dimensions={0}, use_global_device_ids=true | all-gather | bytes 86400 | tf_op jit(solution)/shard_map/all_gather | solution.py:93
  78.5 0.8 reshape.191
  79.3 0.0 all-gather.13.cloned.1.call-update
  79.3 0.0 all-gather.11.cloned.1.call-start
  79.3 1.5 convert_element_type.147
  80.9 0.0 all-gather.11.cloned.1.call-update
  80.9 0.0 all-gather.9.cloned.1.call-start
  81.6 1.1 fusion.12
  82.8 0.1 fusion.33
  82.9 0.1 multiply_cosine_fusion
  83.0 88.6 %all-gather.15.cloned.1.call-done = bf16[64,20,1280]{2,1,0:T(8,128)(2,1)} async-done(((bf16[1,20,1280]{2,1,0:T(8,128)(2,1)}), bf16[64,20,1280]{2,1,0:T(8,128)(2,1)}) %all-gather.15.cloned.1.call-update) | async-done | bytes 3276816 | tf_op jit(solution)/shard_map/all_gather | solution.py:100
  171.6 6.1 %reshape.197 = bf16[1280,1280]{1,0:T(8,128)(2,1)} reshape(bf16[64,20,1280]{2,1,0:T(8,128)(2,1)} %all-gather.15.cloned.1.call-done) | data formatting | bytes 6553600
  177.7 0.0 copy-start.2
  177.7 0.0 copy-start.3
  177.7 119.4 %all-gather.13.cloned.1.call-done = bf16[64,20,1920]{2,1,0:T(8,128)(2,1)} async-done(((bf16[1,20,1920]{2,1,0:T(8,128)(2,1)}), bf16[64,20,1920]{2,1,0:T(8,128)(2,1)}) %all-gather.13.cloned.1.call-update) | async-done | bytes 4915216 | tf_op jit(solution)/shard_map/all_gather | solution.py:99
  297.1 7.5 %reshape.193 = bf16[1280,1920]{1,0:T(8,128)(2,1)} reshape(bf16[64,20,1920]{2,1,0:T(8,128)(2,1)} %all-gather.13.cloned.1.call-done) | data formatting | bytes 9830400
  304.7 0.0 copy-done.2
  304.7 0.0 copy-done.3
  304.7 4.4 convolution_convert_fusion.1
  309.2 0.1 convert.18
  309.3 0.1 subtract_convert_fusion
  309.4 1.7 fusion.41
  311.1 0.0 copy-start.1
  311.1 1.7 convolution_convert_fusion.2
  312.8 0.6 copy-done.1
  313.4 0.7 multiply_reduce_fusion
  314.2 0.0 copy-done.4
  314.2 0.9 multiply_convert_fusion.1
  315.0 0.0 all-gather.9.cloned.1.call-update
  315.1 0.0 reduce-scatter.2.cloned.1.call-start
  315.1 103.7 %all-gather.11.cloned.1.call-done = bf16[1280,2,448]{2,1,0:T(2,128)(2,1)} async-done(((bf16[20,2,448]{2,1,0:T(2,128)(2,1)}), bf16[1280,2,448]{2,1,0:T(2,128)(2,1)}) %all-gather.11.cloned.1.call-update) | async-done | bytes 2293776 | tf_op jit(solution)/shard_map/all_gather | solution.py:111
  418.8 7.4 %copy.40 = bf16[1280,2,448]{0,2,1:T(8,128)(2,1)} copy(bf16[1280,2,448]{2,1,0:T(2,128)(2,1)} %all-gather.11.cloned.1.call-done) | data formatting | bytes 4587520 | tf_op jit(solution)/shard_map/all_gather | solution.py:111
  426.2 66.2 %all-gather.9.cloned.1.call-done = bf16[1024,1280]{1,0:T(8,128)(2,1)} async-done(((bf16[128,1280]{1,0:T(8,128)(2,1)}), bf16[1024,1280]{1,0:T(8,128)(2,1)}) %all-gather.9.cloned.1.call-update) | async-done | bytes 2621456 | tf_op jit(solution)/shard_map/all_gather | solution.py:107
  492.4 5.0 fusion.1
  497.4 0.0 copy-done
  497.4 3.2 convolution_convert_fusion
  500.6 0.0 reduce-scatter.2.cloned.1.call-update
  500.7 0.8 copy.41
  501.5 89.9 %reduce-scatter.2.cloned.1.call-done = bf16[128,1280]{1,0:T(8,128)(2,1)} async-done(((bf16[1024,1280]{1,0:T(8,128)(2,1)}), bf16[128,1280]{1,0:T(8,128)(2,1)}) %reduce-scatter.2.cloned.1.call-update) | async-done | bytes 327696 | tf_op jit(solution)/shard_map/reduce_scatter | solution.py:115
  591.4 1.8 fusion.15
  (15 shorter events, 0.2 us)
Async XLA Ops:
  7.2 490.2 %copy-start = (bf16[448,1280]{1,0:T(8,128)(2,1)S(1)}, bf16[448,1280]{1,0:T(8,128)(2,1)}, u32[]{:S(2)}) copy-start(bf16[448,1280]{1,0:T(8,128)(2,1)} %param.13) | copy-start | bytes 3440644
  7.2 164.4 %all-gather.15.cloned.1.call-start = ((), (), s32[]{:S(2)}) async-start(), calls=%async_computation.5 | async-start | bytes 3993600 | tf_op jit(solution)/shard_map/all_gather | solution.py:100
  43.4 253.7 %all-gather.13.cloned.1.call-start = ((), (), s32[]{:S(2)}) async-start(), calls=%async_computation.4 | async-start | bytes 5990400 | tf_op jit(solution)/shard_map/all_gather | solution.py:99
  79.3 339.5 %all-gather.11.cloned.1.call-start = ((), (), s32[]{:S(2)}) async-start(), calls=%async_computation.2 | async-start | bytes 2662400 | tf_op jit(solution)/shard_map/all_gather | solution.py:111
  80.9 411.5 %all-gather.9.cloned.1.call-start = ((), (), s32[]{:S(2)}) async-start(), calls=%async_computation.1 | async-start | bytes 2949120 | tf_op jit(solution)/shard_map/all_gather | solution.py:107
  177.7 127.0 %copy-start.2 = (bf16[1,128,1280]{2,1,0:T(8,128)(2,1)S(1)}, bf16[1,128,1280]{2,1,0:T(8,128)(2,1)}, u32[]{:S(2)}) copy-start(bf16[1,128,1280]{2,1,0:T(8,128)(2,1)} %param.8) | copy-start | bytes 983044
  177.7 127.0 %copy-start.3 = (f32[1280]{0:T(1024)S(1)}, f32[1280]{0:T(1024)}, u32[]{:S(2)}) copy-start(f32[1280]{0:T(1024)} %param.14) | copy-start | bytes 15364
  311.1 2.3 copy-start.1
  313.4 0.8 copy-start.4
  315.1 276.3 %reduce-scatter.2.cloned.1.call-start = ((), (), s32[]{:S(2)}) async-start(), calls=%async_computation.3 | async-start | bytes 2949120 | tf_op jit(solution)/shard_map/reduce_scatter | solution.py:115
Sparse Core Ops, SparseCore 0:
  43.5 128.0 all-gather.14
  174.3 122.7 all-gather.12
  299.3 119.4 all-gather.10
  422.4 69.9 all-gather.8
  500.7 90.5 reduce-scatter.1
where the time goes:
time: 601 us; the launch traced here: 600 us
  waiting for transfers between devices  468 us (78%)
  blocking collectives  68.8 us (11%)
  local copies, waits for them, and re-layouts  24.2 us (4%)
  matrix products  16.7 us (3%)
  between operations  14.6 us (2%)
  other arithmetic  7.37 us (1%)
    all_gather x1, waiting for transfers between devices, shards(): lax.all_gather(qkv_columns, 'group', axis=0, tiled=True)  119 us
    all_gather x1, waiting for transfers between devices, shards(): lax.all_gather(gate_up_master.astype(jnp.bfloat16), 'group', axis=0, tile...  104 us
    reduce_scatter x1, waiting for transfers between devices, shards(): lax.psum_scatter(jnp.dot(hidden_units, down_weight, preferred_element_typ...  89.9 us
    all_gather x1, waiting for transfers between devices, shards(): lax.all_gather(out_columns, 'group', axis=0, tiled=True)  88.6 us
    all_gather x1, waiting for transfers between devices, shards(): gathered_mid = lax.all_gather(normed_mid, 'shard', axis=0, tiled=True)  66.2 us
    all_gather x1, blocking collectives, shards(): lax.all_gather(out_master.astype(jnp.bfloat16), 'shard', axis=1, tiled=True)  34.6 us
    all_gather x1, blocking collectives, shards(): lax.all_gather(qkv_master.astype(jnp.bfloat16), 'shard', axis=1, tiled=True)  34.2 us
    unnamed x15, local copies, waits for them, and re-layouts  16.7 us
  transfers between devices with their start and end apart: 5, of which 5 were waited for; matrix products, arithmetic and copies ran while one was open for 6% of the time, Pallas kernels for 0%

commit v1 on v0

--- a/solution.py
+++ b/solution.py
@@ -104,7 +104,9 @@
     attended, rotated_keys, value_rows = attention(query_key_value, length)
     middle = stream + jnp.dot(attended, w_out, preferred_element_type=jnp.float32)
     normed_mid = norm_rows(middle, mlp_gain).astype(jnp.bfloat16)
-    gathered_mid = lax.all_gather(normed_mid, "shard", axis=0, tiled=True)
+    gathered_mid = jnp.concatenate(
+        lax.all_to_all(jnp.stack([normed_mid] * lax.axis_size("shard")), "shard", 0, 0), axis=0
+    )
     units = gate_up_master.shape[2]
     summed_units = fold_units(
         gathered_mid,

time: 601 us -> 533 us (0.89)
  the two profiles are of different devices: /device:TPU:32 before, /device:TPU:8 now
where the time goes in v1:
time: 533 us; the launch traced here: 532 us
  waiting for transfers between devices  389 us (73%)
  blocking collectives  71.6 us (13%)
  local copies, waits for them, and re-layouts  25.9 us (5%)
  matrix products  16.7 us (3%)
  between operations  14.6 us (3%)
  starting transfers between devices  7.21 us (1%)
  other arithmetic  6.65 us (1%)
    all_gather x1, waiting for transfers between devices, shards(): lax.all_gather(qkv_columns, 'group', axis=0, tiled=True)  120 us
    all_gather x1, waiting for transfers between devices, shards(): lax.all_gather(gate_up_master.astype(jnp.bfloat16), 'group', axis=0, tile...  95.5 us
    reduce_scatter x1, waiting for transfers between devices, shards(): lax.psum_scatter(jnp.dot(hidden_units, down_weight, preferred_element_typ...  87.7 us
    all_gather x1, waiting for transfers between devices, shards(): lax.all_gather(out_columns, 'group', axis=0, tiled=True)  86 us
    all_gather x1, blocking collectives, shards(): lax.all_gather(out_master.astype(jnp.bfloat16), 'shard', axis=1, tiled=True)  37.4 us
    all_gather x1, blocking collectives, shards(): lax.all_gather(qkv_master.astype(jnp.bfloat16), 'shard', axis=1, tiled=True)  34.3 us
    unnamed x15, local copies, waits for them, and re-layouts  16.6 us
  transfers between devices with their start and end apart: 5, of which 4 were waited for; matrix products, arithmetic and copies ran while one was open for 7% of the time, Pallas kernels for 0%

profile of v1, /device:TPU:8, one launch (start us, length us, event | category | flops | bytes accessed | tf_op | source)
XLA Modules:
  0.0 531.7 jit_solution(4253616202569571463)
XLA Ops:
  7.2 0.0 copy-start
  7.2 0.0 all-gather.12.cloned.1.call-start
  7.2 0.8 convert_bitcast_fusion
  8.1 37.4 %all-gather.2 = bf16[8,160,20]{1,2,0:T(8,128)(2,1)S(1)} all-gather(bf16[1,160,20]{1,2,0:T(8,128)(2,1)S(1)} %convert_bitcast_fusion), channel_id=1, replica_groups=mesh['group'=64,'shard'=8] {'shard'}, dimensions={0}, use_global_device_ids=true | all-gather | bytes 57600 | tf_op jit(solution)/shard_map/all_gather | solution.py:94
  45.4 0.8 reshape.201
  46.2 0.0 all-gather.12.cloned.1.call-update
  46.2 0.0 all-gather.10.cloned.1.call-start
  46.3 0.7 convert_bitcast_fusion.1
  47.0 34.3 %all-gather = bf16[8,240,20]{1,2,0:T(8,128)(2,1)S(1)} all-gather(bf16[1,240,20]{1,2,0:T(8,128)(2,1)S(1)} %convert_bitcast_fusion.1), channel_id=1, replica_groups=mesh['group'=64,'shard'=8] {'shard'}, dimensions={0}, use_global_device_ids=true | all-gather | bytes 86400 | tf_op jit(solution)/shard_map/all_gather | solution.py:93
  81.3 0.8 reshape.197
  82.1 0.0 all-gather.10.cloned.1.call-update
  82.1 0.0 all-gather.8.cloned.1.call-start
  82.2 1.5 convert_element_type.147
  83.7 0.0 all-gather.8.cloned.1.call-update
  83.8 1.1 fusion.11
  85.6 0.1 fusion.32
  85.7 0.1 multiply_cosine_fusion
  85.8 86.0 %all-gather.12.cloned.1.call-done = bf16[64,20,1280]{2,1,0:T(8,128)(2,1)} async-done(((bf16[1,20,1280]{2,1,0:T(8,128)(2,1)}), bf16[64,20,1280]{2,1,0:T(8,128)(2,1)}) %all-gather.12.cloned.1.call-update) | async-done | bytes 3276816 | tf_op jit(solution)/shard_map/all_gather | solution.py:100
  171.8 6.1 %reshape.203 = bf16[1280,1280]{1,0:T(8,128)(2,1)} reshape(bf16[64,20,1280]{2,1,0:T(8,128)(2,1)} %all-gather.12.cloned.1.call-done) | data formatting | bytes 6553600
  177.9 0.0 copy-start.3
  177.9 119.7 %all-gather.10.cloned.1.call-done = bf16[64,20,1920]{2,1,0:T(8,128)(2,1)} async-done(((bf16[1,20,1920]{2,1,0:T(8,128)(2,1)}), bf16[64,20,1920]{2,1,0:T(8,128)(2,1)}) %all-gather.10.cloned.1.call-update) | async-done | bytes 4915216 | tf_op jit(solution)/shard_map/all_gather | solution.py:99
  297.7 7.5 %reshape.199 = bf16[1280,1920]{1,0:T(8,128)(2,1)} reshape(bf16[64,20,1920]{2,1,0:T(8,128)(2,1)} %all-gather.10.cloned.1.call-done) | data formatting | bytes 9830400
  305.2 0.0 copy-done.2
  305.2 0.0 copy-done.3
  305.2 4.4 convolution_convert_fusion.1
  309.7 0.1 convert.18
  309.8 0.1 subtract_convert_fusion
  309.9 1.7 fusion.40
  311.6 0.0 copy-start.1
  311.6 1.7 convolution_convert_fusion.2
  313.3 0.6 copy-done.1
  314.0 0.0 copy-start.4
  314.0 0.7 multiply_reduce_fusion
  314.7 0.0 copy-done.4
  314.7 0.1 multiply_convert_fusion.1
  314.9 1.7 stack.2
  316.5 7.1 %all-to-all-start = ((bf16[8,128,1280]{2,1,0:T(8,128)(2,1)}), bf16[8,128,1280]{2,1,0:T(8,128)(2,1)}, u32[]{:S(2)}, u32[]{:S(2)}) async-start(bf16[8,128,1280]{2,1,0:T(8,128)(2,1)} %stack.2), calls=%async_computation | async-start | bytes 5242880 | tf_op jit(solution)/shard_map/all_to_all | solution.py:108
  323.6 0.0 reduce-scatter.2.cloned.1.call-start
  323.6 95.5 %all-gather.8.cloned.1.call-done = bf16[1280,2,448]{2,1,0:T(2,128)(2,1)} async-done(((bf16[20,2,448]{2,1,0:T(2,128)(2,1)}), bf16[1280,2,448]{2,1,0:T(2,128)(2,1)}) %all-gather.8.cloned.1.call-update) | async-done | bytes 2293776 | tf_op jit(solution)/shard_map/all_gather | solution.py:113
  419.1 7.5 %copy.40 = bf16[1280,2,448]{0,2,1:T(8,128)(2,1)} copy(bf16[1280,2,448]{2,1,0:T(2,128)(2,1)} %all-gather.8.cloned.1.call-done) | data formatting | bytes 4587520 | tf_op jit(solution)/shard_map/all_gather | solution.py:113
  426.6 0.0 all-to-all-done
  426.6 5.0 fusion.1
  431.6 0.0 copy-done
  431.6 3.2 convolution_convert_fusion
  434.8 0.0 reduce-scatter.2.cloned.1.call-update
  434.9 0.8 copy.41
  435.7 87.7 %reduce-scatter.2.cloned.1.call-done = bf16[128,1280]{1,0:T(8,128)(2,1)} async-done(((bf16[1024,1280]{1,0:T(8,128)(2,1)}), bf16[128,1280]{1,0:T(8,128)(2,1)}) %reduce-scatter.2.cloned.1.call-update) | async-done | bytes 327696 | tf_op jit(solution)/shard_map/reduce_scatter | solution.py:117
  523.4 1.8 fusion.14
  (15 shorter events, 0.2 us)
Async XLA Ops:
  7.2 424.4 %copy-start = (bf16[448,1280]{1,0:T(8,128)(2,1)S(1)}, bf16[448,1280]{1,0:T(8,128)(2,1)}, u32[]{:S(2)}) copy-start(bf16[448,1280]{1,0:T(8,128)(2,1)} %param.13) | copy-start | bytes 3440644
  7.2 164.7 %all-gather.12.cloned.1.call-start = ((), (), s32[]{:S(2)}) async-start(), calls=%async_computation.5 | async-start | bytes 3993600 | tf_op jit(solution)/shard_map/all_gather | solution.py:100
  46.2 251.5 %all-gather.10.cloned.1.call-start = ((), (), s32[]{:S(2)}) async-start(), calls=%async_computation.4 | async-start | bytes 5990400 | tf_op jit(solution)/shard_map/all_gather | solution.py:99
  82.1 337.0 %all-gather.8.cloned.1.call-start = ((), (), s32[]{:S(2)}) async-start(), calls=%async_computation.2 | async-start | bytes 2662400 | tf_op jit(solution)/shard_map/all_gather | solution.py:113
  177.9 127.3 %copy-start.2 = (bf16[1,128,1280]{2,1,0:T(8,128)(2,1)S(1)}, bf16[1,128,1280]{2,1,0:T(8,128)(2,1)}, u32[]{:S(2)}) copy-start(bf16[1,128,1280]{2,1,0:T(8,128)(2,1)} %param.8) | copy-start | bytes 983044
  177.9 127.3 %copy-start.3 = (f32[1280]{0:T(1024)S(1)}, f32[1280]{0:T(1024)}, u32[]{:S(2)}) copy-start(f32[1280]{0:T(1024)} %param.14) | copy-start | bytes 15364
  311.6 2.3 copy-start.1
  314.0 0.8 copy-start.4
  316.5 110.0 %all-to-all-start = ((bf16[8,128,1280]{2,1,0:T(8,128)(2,1)}), bf16[8,128,1280]{2,1,0:T(8,128)(2,1)}, u32[]{:S(2)}, u32[]{:S(2)}) async-start(bf16[8,128,1280]{2,1,0:T(8,128)(2,1)} %stack.2), calls=%async_computation | async-start | bytes 5242880 | tf_op jit(solution)/shard_map/all_to_all | solution.py:108
  323.6 199.8 %reduce-scatter.2.cloned.1.call-start = ((), (), s32[]{:S(2)}) async-start(), calls=%async_computation.3 | async-start | bytes 2949120 | tf_op jit(solution)/shard_map/reduce_scatter | solution.py:117
Sparse Core Ops, SparseCore 0:
  46.3 125.4 all-gather.11
  174.6 123.0 all-gather.9
  299.9 119.2 all-gather.7
  434.9 88.4 reduce-scatter.1
